TPU v7x, 32 devices: a whole 2x2x4 slice. The times are simulated.
32 devices in a mesh: dp: 16 (over z, y, x), rep: 2 (over core).
Axes of the slice: x: 2, y: 2, z: 4, core: 2. Of those that a mesh axis runs over, the one named last changes fastest.
Arguments:
- hidden_old: bfloat16 [8192, 6144], P(('dp', 'rep')), may hold values from -400 to 400
- cotangent: bfloat16 [8192, 128], P(('dp', 'rep')), may hold values from -0.15625 to 0.15625
- gain_old: float32 [6144], replicated, may hold values from 0.1 to 1.9
- old_bounds: int32 [17], replicated, may hold values from 0 to 6144, as said below
- new_bounds: int32 [17], replicated, may hold values from 0 to 8192, as said below
- source_map: int32 [8192], replicated, may hold values from 0 to 6143, as said below
- weight_old: bfloat16 [8192, 128], P('dp'), may hold values from -0.078125 to 0.078125
- moment_first: float32 [8192, 128], P('dp'), may hold values from -6 to 6
- moment_second: float32 [8192, 128], P('dp'), may hold values from 0.25 to 4
Outputs:
- projected: bfloat16 [8192, 128], P(('dp', 'rep'))
- gain_grad: float32 [8192], replicated
- first_next: float32 [10240, 128], P('dp')
- second_next: float32 [10240, 128], P('dp')
- adam_step: float32 [10240, 128], P('dp')
Inputs may be any that keep to these rules, and one draw needn't show every extreme that they name: old_bounds[0] = 0, old_bounds[16] = 6144; device p holds old units old_bounds[p] to old_bounds[p+1] - 1, between 256 and 512 of them, exactly 512 on some device. new_bounds[0] = 0, new_bounds[16] = 8192; device q holds new units new_bounds[q] to new_bounds[q+1] - 1, between 384 and 640 of them, exactly 640 on some device. `source_map`: the s-th new unit of a device (counted from its first) copies an old unit held by old device (s + c) mod 16, with an offset c of that new device; so at most 40 new units of one device copy units of one old device, and some pair of devices reaches 40.
All inputs are finite; a program needn't handle non-finite values.
Results may differ from a plain program's by a relative error of at most 0.0049.
Values may be sent and summed in bfloat16 or wider, within the bound.
No kernel may reach another device: no remote copies, remote signals or barrier semaphores. Data moves between devices by JAX's collectives and lax.ppermute only.
A program may use at most 64 MiB of HBM per device.

v0:
```python
import jax
import jax.numpy as jnp
from jax import lax
from jax.sharding import PartitionSpec as P

D_OLD = 6144
D_NEW = 8192


def owners(bounds, unit_ids):
    return jnp.sum((bounds[None, 1:] <= unit_ids[:, None]).astype(jnp.int32), axis=1)


def routing(
    owner_of,
    local_of,
    table_rows,
    slot_cap,
    dev_index,
    dest_owner,
    new_bounds,
    positions,
    wanted,
    own_slots,
    dp_count,
):
    from_me = (owner_of == dev_index).astype(jnp.int32)
    before = jnp.cumsum(from_me) - from_me
    send_slot = before - before[new_bounds[dest_owner]]
    target = jnp.where(from_me > 0, dest_owner * slot_cap + send_slot, dp_count * slot_cap)
    chosen = jnp.zeros((dp_count * slot_cap,), jnp.int32).at[target].set(positions, mode="drop")
    filled = jnp.zeros((dp_count * slot_cap,), jnp.bool_).at[target].set(True, mode="drop")
    local_row = jnp.clip(local_of[chosen], 0, table_rows - 1)
    anchor = owner_of[wanted]
    earlier = (own_slots[None, :] < own_slots[:, None]) & (anchor[None, :] == anchor[:, None])
    arrival_rank = jnp.sum(earlier.astype(jnp.int32), axis=1)
    incoming = jnp.minimum(anchor * slot_cap + arrival_rank, dp_count * slot_cap - 1)
    return (local_row, filled, incoming)


def outgoing(source_table, route_info):
    return jnp.where(
        route_info[1][:, None], source_table[route_info[0]], jnp.zeros((), source_table.dtype)
    )


def arrived(source_table, route_info, live_new):
    return jnp.where(live_new[:, None], source_table[route_info[2]], 0.0)


def on_device(
    hidden_old,
    cotangent,
    gain_old,
    old_bounds,
    new_bounds,
    source_map,
    weight_old,
    moment_first,
    moment_second,
):
    dp_count = lax.axis_size("dp")
    dev_index = lax.axis_index("dp")
    old_cap = weight_old.shape[0]
    new_mean = D_NEW // dp_count
    new_cap = new_mean + new_mean // 4
    pair_cap = (new_cap + dp_count - 1) // dp_count
    positions = jnp.arange(D_NEW, dtype=jnp.int32)
    first_use = jnp.full((D_OLD,), D_NEW, jnp.int32).at[source_map].min(positions)
    unit_used = first_use < D_NEW
    keep_mask = first_use[source_map] == positions
    copies = jnp.zeros((D_OLD,), jnp.float32).at[source_map].add(1.0)
    padded = jnp.arange(dp_count * old_cap, dtype=jnp.int32)
    slot_owner = padded // old_cap
    within = padded - slot_owner * old_cap
    live_old = within < old_bounds[slot_owner + 1] - old_bounds[slot_owner]
    slot_unit = jnp.minimum(old_bounds[slot_owner] + within, D_OLD - 1)
    weight_live = live_old & unit_used[slot_unit]
    source_owner = owners(old_bounds, source_map)
    source_slot = source_owner * old_cap + source_map - old_bounds[source_owner]
    dest_owner = owners(new_bounds, positions)
    own_slots = jnp.arange(new_cap, dtype=jnp.int32)
    live_new = own_slots < new_bounds[dev_index + 1] - new_bounds[dev_index]
    wanted = jnp.minimum(new_bounds[dev_index] + own_slots, D_NEW - 1)
    grad_route = routing(
        source_owner,
        source_map - old_bounds[dev_index],
        old_cap,
        pair_cap,
        dev_index,
        dest_owner,
        new_bounds,
        positions,
        wanted,
        own_slots,
        dp_count,
    )
    moment_route = routing(
        source_owner,
        source_map - old_bounds[dev_index],
        old_cap,
        pair_cap,
        dev_index,
        dest_owner,
        new_bounds,
        positions,
        wanted,
        own_slots,
        dp_count,
    )
    stream = hidden_old.astype(jnp.float32)
    squares = jnp.sum(stream * stream * copies, axis=1)
    inv_rms = lax.rsqrt(squares / D_NEW + 1e-05)
    normed = (stream * inv_rms[:, None] * gain_old).astype(jnp.bfloat16)
    normed_slots = jnp.take(normed, slot_unit, axis=1)
    hidden_slots = jnp.take(hidden_old, slot_unit, axis=1)
    weight_block = lax.all_gather(weight_old, "dp", axis=0, tiled=True)
    masked_block = jnp.where(weight_live[:, None], weight_block, jnp.zeros((), weight_block.dtype))
    columns = normed_slots
    key_sums = jnp.dot(columns, masked_block, preferred_element_type=jnp.float32)
    slopes = lax.dot_general(
        cotangent, masked_block, (((1,), (1,)), ((), ())), preferred_element_type=jnp.float32
    )
    scaled = hidden_slots.astype(jnp.float32) * inv_rms[:, None]
    column_terms = jnp.sum(slopes * scaled, axis=0)
    key_sums, column_terms = (key_sums, column_terms)
    projected = key_sums.astype(jnp.bfloat16)
    columns = normed_slots
    grad_own = lax.psum_scatter(
        lax.dot_general(
            columns, cotangent, (((0,), (0,)), ((), ())), preferred_element_type=jnp.float32
        ),
        "dp",
        scatter_dimension=0,
        tiled=True,
    )
    grad_own = lax.psum(grad_own.astype(jnp.bfloat16), "rep").astype(jnp.float32)
    column_total = lax.psum(column_terms, ("dp", "rep"))
    gain_grad = jnp.where(keep_mask, column_total[source_slot], 0.0)
    moved_grad, moved_first, moved_second = (
        lax.all_to_all(
            outgoing(grad_own, grad_route), "dp", split_axis=0, concat_axis=0, tiled=True
        ),
        lax.all_to_all(
            outgoing(moment_first, moment_route), "dp", split_axis=0, concat_axis=0, tiled=True
        ),
        lax.all_to_all(
            outgoing(moment_second, moment_route), "dp", split_axis=0, concat_axis=0, tiled=True
        ),
    )
    grad_new = arrived(moved_grad, grad_route, live_new)
    first_next = jnp.where(
        live_new[:, None], 0.9 * arrived(moved_first, moment_route, live_new) + 0.1 * grad_new, 0.0
    )
    second_next = jnp.where(
        live_new[:, None],
        0.95 * arrived(moved_second, moment_route, live_new) + 0.05 * grad_new * grad_new,
        0.0,
    )
    adam_step = first_next / (jnp.sqrt(second_next) + 1e-08)
    return (projected, gain_grad, first_next, second_next, adam_step)


def solution(mesh):
    placed = (
        P(("dp", "rep"), None),
        P(("dp", "rep"), None),
        P(),
        P(),
        P(),
        P(),
        P("dp", None),
        P("dp", None),
        P("dp", None),
    )
    return jax.shard_map(
        on_device,
        mesh=mesh,
        in_specs=placed,
        out_specs=(P(("dp", "rep"), None), P(), P("dp", None), P("dp", None), P("dp", None)),
        check_vma=False,
    )
```

profile of v0, /device:TPU:0, one launch (start us, length us, event | category | flops | bytes accessed | tf_op | source)
XLA Modules:
  0.0 749.6 jit_solution(12491640202311818620)
XLA Ops:
  9.9 4.5 compare_select_fusion.25
  14.4 6.3 compare_and_fusion
  20.7 3.2 copy.20
  25.8 44.6 %scatter_custom_fusion = f32[6144]{0:T(1024)} fusion(s32[8192]{0:T(1024)} %get-tuple-element.42, f32[8192]{0:T(1024)} %broadcast.609, f32[]{:T(128)} %constant.37.clone.1), kind=kCustom, calls=%fused_computation.165 | custom fusion | flops 8192 | bytes 25088 | tf_op jit(solution)/shard_map/scatter-add | solution.py:72
  72.2 2.9 fusion.4
  75.0 33.2 %gather_fusion.12 = bf16[8192,256]{1,0:T(8,128)(2,1)} fusion(bf16[256,6144]{0,1:T(8,128)(2,1)} %fusion.4, s32[8192]{0:T(1024)S(1)} %broadcast_clamp_fusion.3), kind=kCustom, calls=%fused_computation.clone | custom fusion | bytes 8421376 | tf_op jit(solution)/shard_map/jit(_take)/gather | solution.py:115
  108.2 7.2 fusion.5
  115.5 98.0 %reduce-scatter.2.cloned.1.call-done = f32[512,128]{1,0:T(8,128)} async-done(((f32[8192,128]{1,0:T(8,128)}), f32[512,128]{1,0:T(8,128)}) %reduce-scatter.2.cloned.1.call-update) | async-done | bytes 262160 | tf_op jit(solution)/shard_map/reduce_scatter | solution.py:129
  218.0 4.5 compare_select_fusion.7
  223.5 6.2 select_select_fusion
  237.4 80.7 %gather_fusion.3 = s32[8192]{0:T(1024)} fusion(s32[8192]{0:T(1024)S(1)} %get-tuple-element.31, s32[8192]{0:T(1024)} %broadcast_clamp_fusion), kind=kCustom, calls=%fused_computation.5 | custom fusion | bytes 98304 | tf_op jit(solution)/shard_map/gather | solution.py:29
  318.1 6.1 compare_select_fusion.13
  324.2 30.8 %scatter_custom_fusion.3 = s32[640]{0:T(1024)S(1)} fusion(s32[8192]{0:T(1024)} %bitcast.97, s32[8192]{0:T(1024)S(1)} %iota.49, s32[]{:T(128)} %constant.38.clone.1), kind=kCustom, calls=%fused_computation.178 | custom fusion | bytes 3072 | tf_op jit(solution)/shard_map/scatter | solution.py:31
  355.1 3.9 gather_fusion.4
  361.2 3.2 gather_fusion.10
  364.5 34.7 %scatter_custom_fusion.2 = pred[640]{0:T(1024)(128)(4,1)S(1)} fusion(s32[8192]{0:T(1024)} %bitcast.98, pred[8192]{0:T(1024)(128)(4,1)S(1)} %broadcast.610, pred[]{:T(512)} %constant.95.clone.1), kind=kCustom, calls=%fused_computation.180 | custom fusion | bytes 1152 | tf_op jit(solution)/shard_map/scatter | solution.py:32
  400.6 3.9 gather_fusion.6
  406.4 44.3 %scatter_custom_fusion.1 = s32[6144]{0:T(1024)S(1)} fusion(s32[8192]{0:T(1024)} %get-tuple-element.42, s32[8192]{0:T(1024)} %iota.45, s32[]{:T(128)} %constant.34.clone.1), kind=kCustom, calls=%fused_computation.163 | custom fusion | flops 8192 | bytes 25088 | tf_op jit(solution)/shard_map/scatter-min | solution.py:69
  459.8 3.2 gather_fusion.8
  465.2 5.2 all-to-all-start.2
  471.1 32.9 %gather_fusion.13 = bf16[8192,256]{1,0:T(8,128)(2,1)} fusion(bf16[256,6144]{0,1:T(8,128)(2,1)S(1)} %copy.20, s32[8192]{0:T(1024)S(1)} %copy-done.6), kind=kCustom, calls=%fused_computation.1.clone | custom fusion | bytes 8421376 | tf_op jit(solution)/shard_map/jit(_take)/gather | solution.py:116
  504.1 6.4 copy.22
  510.5 45.5 %gather_fusion.1 = s32[8192]{0:T(1024)S(1)} fusion(s32[6144]{0:T(1024)S(1)} %scatter_custom_fusion.1, s32[8192]{0:T(1024)S(1)} %copy-done.13), kind=kCustom, calls=%fused_computation.3 | custom fusion | bytes 98304 | tf_op jit(solution)/shard_map/gather | solution.py:71
  556.2 50.7 %gather_fusion = pred[8192]{0:T(1024)(128)(4,1)S(1)} fusion(pred[6144]{0:T(1024)(128)(4,1)S(1)} %broadcast_compare_fusion.1, s32[8192]{0:T(1024)S(1)} %copy-done.9), kind=kCustom, calls=%fused_computation.2 | custom fusion | bytes 49152 | tf_op jit(solution)/shard_map/gather | solution.py:78
  608.0 6.3 fusion.25
  614.3 6.3 fusion.22
  620.7 6.9 all-to-all-start
  627.6 7.3 fusion.9
  635.0 40.8 %psum.14 = f32[8192]{0:T(1024)S(1)} all-reduce(f32[8192]{0:T(1024)S(1)} %fusion.9), channel_id=1, replica_groups=mesh['dp'=16,'rep'=2] {'dp','rep'}, use_global_device_ids=true, to_apply=%region_4.6 | all-reduce | flops 8192 | bytes 65536 | tf_op jit(solution)/shard_map/psum | solution.py:138
  675.8 45.5 %gather_fusion.2 = f32[8192]{0:T(1024)S(1)} fusion(f32[8192]{0:T(1024)S(1)} %psum.14, s32[8192]{0:T(1024)S(1)} %fusion.22), kind=kCustom, calls=%fused_computation.4 | custom fusion | bytes 98304 | tf_op jit(solution)/shard_map/gather | solution.py:139
  721.4 5.4 all-to-all-start.1
  727.4 8.4 %fusion.11 = bf16[256,128]{1,0:T(8,128)(2,1)} fusion(bf16[8192,256]{1,0:T(8,128)(2,1)} %gather_fusion.12, pred[8192]{0:T(1024)(128)(4,1)S(1)} %get-tuple-element.37, bf16[8192,128]{1,0:T(8,128)(2,1)S(1)} %copy-done.28, pred[8192]{0:T(1024)(128)(4,1)S(1)} %fusion.25), kind=kOutput, calls=%fused_computation.36 | convolution fusion | flops 540049408 | bytes 6373376 | tf_op jit(solution)/shard_map/dot_general | solution.py:120
  (139 shorter events, 44.6 us)
Async XLA Ops:
  7.2 351.8 %copy-start = (f32[512,128]{1,0:T(8,128)S(1)}, f32[512,128]{1,0:T(8,128)}, u32[]{:S(2)}) copy-start(f32[512,128]{1,0:T(8,128)} %param.18) | copy-start | bytes 786436
  7.2 16.8 %copy-start.2 = (s32[8192]{0:T(1024)S(1)}, s32[8192]{0:T(1024)}, u32[]{:S(2)}) copy-start(s32[8192]{0:T(1024)} %param.16) | copy-start | bytes 98308
  7.2 206.3 %reduce-scatter.2.cloned.1.call-start = ((), (), s32[]{:S(2)}) async-start(), calls=%async_computation.5 | async-start | bytes 4456448 | tf_op jit(solution)/shard_map/reduce_scatter | solution.py:129
  20.7 54.3 %copy-start.5 = (s32[8192]{0:T(1024)}, s32[8192]{0:T(1024)S(1)}, u32[]{:S(2)}) copy-start(s32[8192]{0:T(1024)S(1)} %broadcast_clamp_fusion.3) | copy-start | bytes 98308
  72.2 36.1 %copy-start.25 = (f32[256]{0:T(256)}, f32[256]{0:T(256)S(1)}, u32[]{:S(2)}) copy-start(f32[256]{0:T(256)S(1)} %add_rsqrt_fusion) | copy-start | bytes 3076
  115.4 100.4 %copy-start.8 = (s32[17]{0:T(128)S(1)}, s32[17]{0:T(128)}, u32[]{:S(2)}) copy-start(s32[17]{0:T(128)} %param.15) | copy-start | bytes 208
  115.4 101.1 %copy-start.7 = (s32[17]{0:T(128)S(1)}, s32[17]{0:T(128)}, u32[]{:S(2)}) copy-start(s32[17]{0:T(128)} %param.14) | copy-start | bytes 208
  115.4 342.7 %all-reduce.2.cloned.1.call-start = ((), (), s32[]{:S(2)}) async-start(), calls=%async_computation.6 | async-start | bytes 262144 | tf_op jit(solution)/shard_map/psum | solution.py:137
  215.1 412.5 %all-gather.2.cloned.1.call-start = ((), (), s32[]{:S(2)}) async-start(), calls=%async_computation.4 | async-start | bytes 2228224 | tf_op jit(solution)/shard_map/all_gather | solution.py:117
  218.0 11.8 %copy-start.4 = (s32[8192]{0:T(1024)}, s32[8192]{0:T(1024)S(1)}, u32[]{:S(2)}) copy-start(s32[8192]{0:T(1024)S(1)} %convert_reduce_fusion.1) | copy-start | bytes 98308
  404.4 66.7 %copy-start.6 = (s32[8192]{0:T(1024)S(1)}, s32[8192]{0:T(1024)}, u32[]{:S(2)}) copy-start(s32[8192]{0:T(1024)} %copy-done.5) | copy-start | bytes 98308
  465.2 155.4 %all-to-all-start.2 = ((f32[16,40,128]{2,1,0:T(8,128)}), f32[16,40,128]{2,1,0:T(8,128)}, u32[]{:S(2)}, u32[]{:S(2)}) async-start(f32[16,40,128]{2,1,0:T(8,128)} %get-tuple-element.45), calls=%async_computation.3 | async-start | bytes 655360 | tf_op jit(solution)/shard_map/all_to_all | solution.py:147
  510.4 45.5 %copy-start.9 = (s32[8192]{0:T(1024)S(1)}, s32[8192]{0:T(1024)}, u32[]{:S(2)}) copy-start(s32[8192]{0:T(1024)} %broadcast_clamp_fusion.2) | copy-start | bytes 98308
  556.0 50.9 %copy-start.10 = (s32[8192,1]{0,1:T(1,128)S(1)}, s32[8192,1]{0,1:T(1,128)}, u32[]{:S(2)}) copy-start(s32[8192,1]{0,1:T(1,128)} %get-tuple-element.36) | copy-start | bytes 98308
  556.0 51.9 %copy-start.12 = (s32[8192,1]{0,1:T(1,128)S(1)}, s32[8192,1]{0,1:T(1,128)}, u32[]{:S(2)}) copy-start(s32[8192,1]{0,1:T(1,128)} %get-tuple-element.82) | copy-start | bytes 98308
  556.0 51.9 %copy-start.15 = (pred[8192]{0:T(1024)(128)(4,1)S(1)}, pred[8192]{0:T(1024)(128)(4,1)}, u32[]{:S(2)}) copy-start(pred[8192]{0:T(1024)(128)(4,1)} %compare_reduce_fusion.20) | copy-start | bytes 24580
  556.0 51.9 %copy-start.16 = (pred[8192]{0:T(1024)(128)(4,1)S(1)}, pred[8192]{0:T(1024)(128)(4,1)}, u32[]{:S(2)}) copy-start(pred[8192]{0:T(1024)(128)(4,1)} %compare_reduce_fusion.21) | copy-start | bytes 24580
  556.0 51.9 %copy-start.17 = (pred[8192]{0:T(1024)(128)(4,1)S(1)}, pred[8192]{0:T(1024)(128)(4,1)}, u32[]{:S(2)}) copy-start(pred[8192]{0:T(1024)(128)(4,1)} %compare_reduce_fusion.22) | copy-start | bytes 24580
  556.0 51.9 %copy-start.18 = (pred[8192]{0:T(1024)(128)(4,1)S(1)}, pred[8192]{0:T(1024)(128)(4,1)}, u32[]{:S(2)}) copy-start(pred[8192]{0:T(1024)(128)(4,1)} %compare_reduce_fusion.23) | copy-start | bytes 24580
  556.1 51.9 %copy-start.19 = (pred[8192]{0:T(1024)(128)(4,1)S(1)}, pred[8192]{0:T(1024)(128)(4,1)}, u32[]{:S(2)}) copy-start(pred[8192]{0:T(1024)(128)(4,1)} %compare_reduce_fusion.24) | copy-start | bytes 24580
  556.1 51.9 %copy-start.20 = (pred[8192]{0:T(1024)(128)(4,1)S(1)}, pred[8192]{0:T(1024)(128)(4,1)}, u32[]{:S(2)}) copy-start(pred[8192]{0:T(1024)(128)(4,1)} %compare_reduce_fusion.25) | copy-start | bytes 24580
  556.1 51.9 %copy-start.21 = (pred[8192]{0:T(1024)(128)(4,1)S(1)}, pred[8192]{0:T(1024)(128)(4,1)}, u32[]{:S(2)}) copy-start(pred[8192]{0:T(1024)(128)(4,1)} %compare_reduce_fusion.26) | copy-start | bytes 24580
  556.1 51.9 %copy-start.22 = (pred[8192]{0:T(1024)(128)(4,1)S(1)}, pred[8192]{0:T(1024)(128)(4,1)}, u32[]{:S(2)}) copy-start(pred[8192]{0:T(1024)(128)(4,1)} %compare_reduce_fusion.27) | copy-start | bytes 24580
  556.1 51.9 %copy-start.23 = (pred[8192]{0:T(1024)(128)(4,1)S(1)}, pred[8192]{0:T(1024)(128)(4,1)}, u32[]{:S(2)}) copy-start(pred[8192]{0:T(1024)(128)(4,1)} %compare_reduce_fusion.28) | copy-start | bytes 24580
  556.1 51.9 %copy-start.24 = (pred[8192]{0:T(1024)(128)(4,1)S(1)}, pred[8192]{0:T(1024)(128)(4,1)}, u32[]{:S(2)}) copy-start(pred[8192]{0:T(1024)(128)(4,1)} %compare_reduce_fusion.29) | copy-start | bytes 24580
  556.1 58.2 %copy-start.3 = (s32[8192]{0:T(1024)S(1)}, s32[8192]{0:T(1024)}, u32[]{:S(2)}) copy-start(s32[8192]{0:T(1024)} %param.16) | copy-start | bytes 98308
  556.1 58.2 %copy-start.11 = (s32[8192,1]{0,1:T(1,128)S(1)}, s32[8192,1]{0,1:T(1,128)}, u32[]{:S(2)}) copy-start(s32[8192,1]{0,1:T(1,128)} %get-tuple-element.35) | copy-start | bytes 98308
  556.1 71.5 %copy-start.14 = (bf16[256,128]{1,0:T(8,128)(2,1)S(1)}, bf16[256,128]{1,0:T(8,128)(2,1)}, u32[]{:S(2)}) copy-start(bf16[256,128]{1,0:T(8,128)(2,1)} %param.12) | copy-start | bytes 196612
  556.1 71.5 %copy-start.26 = (f32[256]{0:T(256)S(1)}, f32[256]{0:T(256)}, u32[]{:S(2)}) copy-start(f32[256]{0:T(256)} %copy-done.25) | copy-start | bytes 3076
  620.7 100.7 %all-to-all-start = ((f32[16,40,128]{2,1,0:T(8,128)}), f32[16,40,128]{2,1,0:T(8,128)S(1)}, u32[]{:S(2)}, u32[]{:S(2)}) async-start(f32[16,40,128]{2,1,0:T(8,128)} %get-tuple-element.43), calls=%async_computation | async-start | bytes 655360 | tf_op jit(solution)/shard_map/all_to_all | solution.py:144
  675.8 51.6 %copy-start.28 = (bf16[8192,128]{1,0:T(8,128)(2,1)S(1)}, bf16[8192,128]{1,0:T(8,128)(2,1)}, u32[]{:S(2)}) copy-start(bf16[8192,128]{1,0:T(8,128)(2,1)} %all-gather.2.cloned.1.call-done) | copy-start | bytes 6291460
  721.4 18.7 %all-to-all-start.1 = ((f32[16,40,128]{2,1,0:T(8,128)}), f32[16,40,128]{2,1,0:T(8,128)S(1)}, u32[]{:S(2)}, u32[]{:S(2)}) async-start(f32[16,40,128]{2,1,0:T(8,128)} %get-tuple-element.44), calls=%async_computation.2 | async-start | bytes 655360 | tf_op jit(solution)/shard_map/all_to_all | solution.py:141
  (3 other events, 15.4 us)
Sparse Core Ops, SparseCore 0:
  115.6 97.8 reduce-scatter.1
  216.3 17.4 all-reduce.1
  236.6 61.8 all-gather.1
where the time goes:
time: 752 us; the launch traced here: 750 us
  local copies, waits for them, and re-layouts  394 us (52%)
  other arithmetic  160 us (21%)
  waiting for transfers between devices  98.7 us (13%)
  blocking collectives  40.8 us (5%)
  matrix products  22.9 us (3%)
  starting transfers between devices  17.7 us (2%)
  between operations  15.8 us (2%)
    reduce_scatter x1, waiting for transfers between devices, on_device(): lax.psum_scatter(lax.dot_general(columns, cotangent, (((0,), (0,)), ((),...  98 us
    gather x2, local copies, waits for them, and re-layouts, routing(): send_slot = before - before[new_bounds[dest_owner]]  81.3 us
    gather x1, local copies, waits for them, and re-layouts, on_device(): weight_live = live_old & unit_used[slot_unit]  50.7 us
    gather x1, local copies, waits for them, and re-layouts, on_device(): gain_grad = jnp.where(keep_mask, column_total[source_slot], 0.0)  45.5 us
    gather x1, local copies, waits for them, and re-layouts, on_device(): keep_mask = first_use[source_map] == positions  45.5 us
    scatter-add x1, other arithmetic, on_device(): copies = jnp.zeros((D_OLD,), jnp.float32).at[source_map].add(1.0)  44.6 us
    another operation x1, other arithmetic, on_device(): jnp.full((D_OLD,), D_NEW, jnp.int32).at[source_map].min(positions)  44.3 us
    psum x1, blocking collectives, on_device(): column_total = lax.psum(column_terms, ('dp', 'rep'))  40.8 us
  transfers between devices with their start and end apart: 6, of which 1 were waited for; matrix products, arithmetic and copies ran while one was open for 62% of the time, Pallas kernels for 0%

commit v1 on v0

--- a/solution.py
+++ b/solution.py
@@ -135,7 +135,8 @@
         tiled=True,
     )
     grad_own = lax.psum(grad_own.astype(jnp.bfloat16), "rep").astype(jnp.float32)
-    column_total = lax.psum(column_terms, ("dp", "rep"))
+    then = lax.all_gather(column_terms, ("dp", "rep"))
+    column_total = jnp.sum(then, axis=0)
     gain_grad = jnp.where(keep_mask, column_total[source_slot], 0.0)
     moved_grad, moved_first, moved_second = (
         lax.all_to_all(

time: 752 us -> 625 us (0.83)
  waiting for transfers between devices: 98.7 us -> 20.9 us
  blocking collectives: 40.8 us -> 0 us
  other arithmetic: 160 us -> 150 us
    reduce_scatter x1, waiting for transfers between devices: 98 us -> 0.02 us  [on_device(): lax.psum_scatter(lax.dot_general(columns, cotangent, (((0,), (0,)), ((),...]
    psum x1 -> x0, blocking collectives: 40.8 us -> none  [on_device(): column_total = lax.psum(column_terms, ('dp', 'rep'))]
    psum x1, waiting for transfers between devices: 0.01 us -> 12.7 us  [on_device(): lax.psum(grad_own.astype(jnp.bfloat16), 'rep').astype(jnp.float32)]
  transfers between devices with their start and end apart: 6 -> 7, of which waited for: 1 -> 2; matrix products, arithmetic and copies ran while one was open for 62% -> 73% of each run, Pallas kernels for 0% -> 0%
where the time goes in v1:
time: 625 us; the launch traced here: 622 us
  local copies, waits for them, and re-layouts  392 us (63%)
  other arithmetic  150 us (24%)
  matrix products  25.4 us (4%)
  waiting for transfers between devices  20.9 us (3%)
  starting transfers between devices  17.4 us (3%)
  between operations  15.6 us (2%)
    gather x2, local copies, waits for them, and re-layouts, routing(): send_slot = before - before[new_bounds[dest_owner]]  81.2 us
    gather x1, local copies, waits for them, and re-layouts, on_device(): weight_live = live_old & unit_used[slot_unit]  50.7 us
    gather x1, local copies, waits for them, and re-layouts, on_device(): keep_mask = first_use[source_map] == positions  45.5 us
    gather x1, local copies, waits for them, and re-layouts, on_device(): gain_grad = jnp.where(keep_mask, column_total[source_slot], 0.0)  45.5 us
    scatter-add x1, other arithmetic, on_device(): copies = jnp.zeros((D_OLD,), jnp.float32).at[source_map].add(1.0)  44.6 us
    another operation x1, other arithmetic, on_device(): jnp.full((D_OLD,), D_NEW, jnp.int32).at[source_map].min(positions)  44.4 us
    gather x2, local copies, waits for them, and re-layouts, on_device(): hidden_slots = jnp.take(hidden_old, slot_unit, axis=1)  41.9 us
    scatter x1, local copies, waits for them, and re-layouts, routing(): jnp.zeros((dp_count * slot_cap,), jnp.bool_).at[target]  34.7 us
  transfers between devices with their start and end apart: 7, of which 2 were waited for; matrix products, arithmetic and copies ran while one was open for 73% of the time, Pallas kernels for 0%

profile of v1, /device:TPU:0, one launch (start us, length us, event | category | flops | bytes accessed | tf_op | source)
XLA Modules:
  0.0 622.0 jit_solution(15385956993078225056)
XLA Ops:
  7.8 2.0 fusion.43
  9.8 4.4 compare_select_fusion.25
  14.3 6.3 %compare_and_fusion = (pred[8192]{0:T(1024)(128)(4,1)S(1)}, s32[8192]{0:T(1024)S(1)}) fusion(pred[8192]{0:T(1024)(128)(4,1)S(1)} %compare_reduce_fusion.30, pred[8192]{0:T(1024)(128)(4,1)S(1)} %compare_reduce_fusion.31, pred[8192]{0:T(1024)(128)(4,1)S(1)} %compare_reduce_fusion.32, pred[8192]{0:T(1024)(128)(4,1)S(1)} %compare_reduce_fusion.33, ...), kind=kLoop, calls=%fused_computation.150 | loop fusion | flops 229376 | bytes 155688 | tf_op jit(solution)/shard_map/jit(_take)/and | solution.py:115
  20.6 3.2 copy.23
  25.7 44.6 %scatter_custom_fusion = f32[6144]{0:T(1024)} fusion(s32[8192]{0:T(1024)} %get-tuple-element.42, f32[8192]{0:T(1024)} %broadcast.609, f32[]{:T(128)} %constant.37.clone.1), kind=kCustom, calls=%fused_computation.165 | custom fusion | flops 8192 | bytes 25088 | tf_op jit(solution)/shard_map/scatter-add | solution.py:72
  70.4 1.7 fusion.2
  72.6 2.9 fusion.4
  75.5 33.2 %gather_fusion.12 = bf16[8192,256]{1,0:T(8,128)(2,1)} fusion(bf16[256,6144]{0,1:T(8,128)(2,1)} %fusion.4, s32[8192]{0:T(1024)S(1)} %broadcast_clamp_fusion.3), kind=kCustom, calls=%fused_computation.clone | custom fusion | bytes 8421376 | tf_op jit(solution)/shard_map/jit(_take)/gather | solution.py:115
  108.7 7.2 %fusion.5 = f32[8192,128]{1,0:T(8,128)} fusion(bf16[256,128]{1,0:T(8,128)(2,1)} %param.12, bf16[8192,256]{1,0:T(8,128)(2,1)} %gather_fusion.12, pred[8192]{0:T(1024)(128)(4,1)S(1)} %get-tuple-element.37), kind=kOutput, calls=%fused_computation.26 | convolution fusion | flops 538968064 | bytes 8462336 | tf_op jit(solution)/shard_map/dot_general | solution.py:130
  118.9 4.4 compare_select_fusion.7
  124.3 6.2 %select_select_fusion = s32[8192]{0:T(1024)S(1)} fusion(pred[8192]{0:T(1024)(128)(4,1)S(1)} %get-tuple-element.15, pred[8192]{0:T(1024)(128)(4,1)S(1)} %get-tuple-element.14, pred[8192]{0:T(1024)(128)(4,1)S(1)} %get-tuple-element.13, pred[8192]{0:T(1024)(128)(4,1)S(1)} %get-tuple-element.12, pred[8192]{0:T(1024)(128)(4,1)S(1)} %get-tuple-element.11, ...), kind=kLoop, calls=%fused_computation.143 | loop fusion | flops 81920 | bytes 147496 | tf_op jit(solution)/shard_map/gather | solution.py:29
  137.5 80.7 %gather_fusion.3 = s32[8192]{0:T(1024)} fusion(s32[8192]{0:T(1024)S(1)} %get-tuple-element.31, s32[8192]{0:T(1024)} %broadcast_clamp_fusion), kind=kCustom, calls=%fused_computation.5 | custom fusion | bytes 98304 | tf_op jit(solution)/shard_map/gather | solution.py:29
  218.2 6.1 compare_select_fusion.13
  224.3 35.6 %gather_fusion.13 = bf16[8192,256]{1,0:T(8,128)(2,1)} fusion(bf16[256,6144]{0,1:T(8,128)(2,1)S(1)} %copy.23, s32[8192]{0:T(1024)} %copy-done.6), kind=kCustom, calls=%fused_computation.1.clone | custom fusion | bytes 8421376 | tf_op jit(solution)/shard_map/jit(_take)/gather | solution.py:116
  259.9 30.9 %scatter_custom_fusion.3 = s32[640]{0:T(1024)S(1)} fusion(s32[8192]{0:T(1024)} %bitcast.98, s32[8192]{0:T(1024)S(1)} %iota.49, s32[]{:T(128)} %constant.38.clone.1), kind=kCustom, calls=%fused_computation.178 | custom fusion | bytes 3072 | tf_op jit(solution)/shard_map/scatter | solution.py:31
  290.8 3.9 gather_fusion.4
  298.1 34.7 %scatter_custom_fusion.2 = pred[640]{0:T(1024)(128)(4,1)S(1)} fusion(s32[8192]{0:T(1024)} %bitcast.99, pred[8192]{0:T(1024)(128)(4,1)S(1)} %broadcast.610, pred[]{:T(512)} %constant.95.clone.1), kind=kCustom, calls=%fused_computation.180 | custom fusion | bytes 1152 | tf_op jit(solution)/shard_map/scatter | solution.py:32
  332.9 6.4 %copy.25 = bf16[8192,256]{0,1:T(8,128)(2,1)} copy(bf16[8192,256]{1,0:T(8,128)(2,1)} %gather_fusion.13) | data formatting | bytes 8388608 | tf_op jit(solution)/shard_map/jit(_take)/gather | solution.py:116
  339.3 44.4 %scatter_custom_fusion.1 = s32[6144]{0:T(1024)S(1)} fusion(s32[8192]{0:T(1024)} %get-tuple-element.42, s32[8192]{0:T(1024)S(1)} %iota.45, s32[]{:T(128)} %constant.34.clone.1), kind=kCustom, calls=%fused_computation.163 | custom fusion | flops 8192 | bytes 25088 | tf_op jit(solution)/shard_map/scatter-min | solution.py:69
  383.8 50.7 %gather_fusion = pred[8192]{0:T(1024)(128)(4,1)S(1)} fusion(pred[6144]{0:T(1024)(128)(4,1)S(1)} %broadcast_compare_fusion.1, s32[8192]{0:T(1024)S(1)} %broadcast_clamp_fusion.2), kind=kCustom, calls=%fused_computation.2 | custom fusion | bytes 49152 | tf_op jit(solution)/shard_map/gather | solution.py:78
  435.1 6.3 %fusion.25 = pred[8192]{0:T(1024)(128)(4,1)S(1)} fusion(pred[8192]{0:T(1024)(128)(4,1)S(1)} %gather_fusion, s32[8192]{0:T(1024)S(1)} %get-tuple-element.38, pred[8192]{0:T(1024)(128)(4,1)S(1)} %compare_reduce_fusion.20, pred[8192]{0:T(1024)(128)(4,1)S(1)} %compare_reduce_fusion.21, pred[8192]{0:T(1024)(128)(4,1)S(1)} %compare_reduce_fusion.22, ...), kind=kLoop, calls=%fused_computation.151 | loop fusion | flops 188416 | bytes 163880 | tf_op jit(solution)/shard_map/and | solution.py:78
  443.2 7.9 %fusion.9 = f32[8192]{0:T(1024)} fusion(f32[256]{0:T(256)S(1)} %copy-done.14, bf16[8192,256]{0,1:T(8,128)(2,1)} %copy.25, pred[8192]{0:T(1024)(128)(4,1)S(1)} %get-tuple-element.37, bf16[256,128]{1,0:T(8,128)(2,1)S(1)} %copy-done.12, bf16[8192,128]{1,0:T(8,128)(2,1)} %all-gather.4.cloned.1.call-done, pred[8192]{0:T(1024)(128)(4,1)S(1)} %fusion.25), kind=kOutput, calls=%fused_computation.31 | convolution fusion | flops 548397056 | bytes 6407168 | tf_op jit(solution)/shard_map/dot_general | solution.py:121
  451.2 12.7 %all-reduce.2.cloned.1.call-done = bf16[512,128]{1,0:T(8,128)(2,1)} async-done(((bf16[512,128]{1,0:T(8,128)(2,1)}), bf16[512,128]{1,0:T(8,128)(2,1)}) %all-reduce.2.cloned.1.call-update) | async-done | bytes 131088 | tf_op jit(solution)/shard_map/psum | solution.py:137
  467.6 6.8 %all-to-all-start.2 = ((f32[16,40,128]{2,1,0:T(8,128)}), f32[16,40,128]{2,1,0:T(8,128)S(1)}, u32[]{:S(2)}, u32[]{:S(2)}) async-start(f32[16,40,128]{2,1,0:T(8,128)} %get-tuple-element.45), calls=%async_computation.3 | async-start | bytes 655360 | tf_op jit(solution)/shard_map/all_to_all | solution.py:148
  475.0 3.9 gather_fusion.6
  479.2 7.4 %all-to-all-done.2 = f32[16,40,128]{2,1,0:T(8,128)S(1)} async-done(((f32[16,40,128]{2,1,0:T(8,128)}), f32[16,40,128]{2,1,0:T(8,128)S(1)}, u32[]{:S(2)}, u32[]{:S(2)}) %all-to-all-start.2) | async-done | bytes 327712 | tf_op jit(solution)/shard_map/all_to_all | solution.py:148
  486.6 3.8 all-to-all-start
  491.7 45.5 %gather_fusion.1 = s32[8192]{0:T(1024)S(1)} fusion(s32[6144]{0:T(1024)S(1)} %scatter_custom_fusion.1, s32[8192]{0:T(1024)S(1)} %copy-done.11), kind=kCustom, calls=%fused_computation.3 | custom fusion | bytes 98304 | tf_op jit(solution)/shard_map/gather | solution.py:71
  538.3 6.3 %fusion.22 = s32[8192]{0:T(1024)S(1)} fusion(pred[8192]{0:T(1024)(128)(4,1)S(1)} %get-tuple-element.25, pred[8192]{0:T(1024)(128)(4,1)S(1)} %get-tuple-element.24, pred[8192]{0:T(1024)(128)(4,1)S(1)} %get-tuple-element.23, pred[8192]{0:T(1024)(128)(4,1)S(1)} %get-tuple-element.22, pred[8192]{0:T(1024)(128)(4,1)S(1)} %get-tuple-element.21, ...), kind=kLoop, calls=%fused_computation.141 | loop fusion | flops 139264 | bytes 213032 | tf_op jit(solution)/shard_map/gather | solution.py:140
  544.6 6.7 %all-to-all-start.1 = ((f32[16,40,128]{2,1,0:T(8,128)}), f32[16,40,128]{2,1,0:T(8,128)S(1)}, u32[]{:S(2)}, u32[]{:S(2)}) async-start(f32[16,40,128]{2,1,0:T(8,128)} %get-tuple-element.44), calls=%async_computation.2 | async-start | bytes 655360 | tf_op jit(solution)/shard_map/all_to_all | solution.py:142
  551.3 10.3 %fusion.11 = bf16[256,128]{1,0:T(8,128)(2,1)} fusion(bf16[8192,256]{1,0:T(8,128)(2,1)} %gather_fusion.12, pred[8192]{0:T(1024)(128)(4,1)S(1)} %get-tuple-element.37, bf16[8192,128]{1,0:T(8,128)(2,1)} %all-gather.4.cloned.1.call-done, pred[8192]{0:T(1024)(128)(4,1)S(1)} %fusion.25), kind=kOutput, calls=%fused_computation.36 | convolution fusion | flops 540049408 | bytes 6373376 | tf_op jit(solution)/shard_map/dot_general | solution.py:120
  563.1 45.5 %gather_fusion.2 = f32[8192]{0:T(1024)S(1)} fusion(f32[8192]{0:T(1024)S(1)} %reduce_sum.64, s32[8192]{0:T(1024)S(1)} %fusion.22), kind=kCustom, calls=%fused_computation.4 | custom fusion | bytes 98304 | tf_op jit(solution)/shard_map/gather | solution.py:140
  (115 shorter events, 33.9 us)
Async XLA Ops:
  7.2 287.6 %copy-start = (f32[512,128]{1,0:T(8,128)S(1)}, f32[512,128]{1,0:T(8,128)}, u32[]{:S(2)}) copy-start(f32[512,128]{1,0:T(8,128)} %param.18) | copy-start | bytes 786436
  7.2 16.7 %copy-start.3 = (s32[8192]{0:T(1024)S(1)}, s32[8192]{0:T(1024)}, u32[]{:S(2)}) copy-start(s32[8192]{0:T(1024)} %param.16) | copy-start | bytes 98308
  7.2 434.3 %reduce-scatter.2.cloned.1.call-start = ((), (), s32[]{:S(2)}) async-start(), calls=%async_computation.5 | async-start | bytes 4456448 | tf_op jit(solution)/shard_map/reduce_scatter | solution.py:129
  20.6 54.9 %copy-start.6 = (s32[8192]{0:T(1024)}, s32[8192]{0:T(1024)S(1)}, u32[]{:S(2)}) copy-start(s32[8192]{0:T(1024)S(1)} %broadcast_clamp_fusion.3) | copy-start | bytes 98308
  72.0 0.6 copy-start.13
  115.9 0.8 copy-start.8
  115.9 1.5 copy-start.7
  115.9 327.3 %all-gather.4.cloned.1.call-start = ((), (), s32[]{:S(2)}) async-start(), calls=%async_computation.4 | async-start | bytes 2228224 | tf_op jit(solution)/shard_map/all_gather | solution.py:117
  116.7 347.2 %all-reduce.2.cloned.1.call-start = ((), (), s32[]{:S(2)}) async-start(), calls=%async_computation.6 | async-start | bytes 262144 | tf_op jit(solution)/shard_map/psum | solution.py:137
  118.3 0.6 copy-start.5
  133.1 3.0 copy-start.2
  259.9 36.6 %copy-start.1 = (f32[512,128]{1,0:T(8,128)S(1)}, f32[512,128]{1,0:T(8,128)}, u32[]{:S(2)}) copy-start(f32[512,128]{1,0:T(8,128)} %param.19) | copy-start | bytes 786436
  383.8 51.3 %copy-start.10 = (s32[8192,1]{0,1:T(1,128)S(1)}, s32[8192,1]{0,1:T(1,128)}, u32[]{:S(2)}) copy-start(s32[8192,1]{0,1:T(1,128)} %get-tuple-element.82) | copy-start | bytes 98308
  383.8 59.4 %copy-start.12 = (bf16[256,128]{1,0:T(8,128)(2,1)S(1)}, bf16[256,128]{1,0:T(8,128)(2,1)}, u32[]{:S(2)}) copy-start(bf16[256,128]{1,0:T(8,128)(2,1)} %param.12) | copy-start | bytes 196612
  383.8 59.4 %copy-start.14 = (f32[256]{0:T(256)S(1)}, f32[256]{0:T(256)}, u32[]{:S(2)}) copy-start(f32[256]{0:T(256)} %copy-done.13) | copy-start | bytes 3076
  443.1 118.4 %all-gather.6.cloned.1.call-start = ((), (), s32[]{:S(2)}) async-start(), calls=%async_computation.7 | async-start | bytes 1081344 | tf_op jit(solution)/shard_map/all_gather | solution.py:138
  466.5 25.2 %copy-start.11 = (s32[8192]{0:T(1024)S(1)}, s32[8192]{0:T(1024)}, u32[]{:S(2)}) copy-start(s32[8192]{0:T(1024)} %get-tuple-element.41) | copy-start | bytes 98308
  467.6 19.1 %all-to-all-start.2 = ((f32[16,40,128]{2,1,0:T(8,128)}), f32[16,40,128]{2,1,0:T(8,128)S(1)}, u32[]{:S(2)}, u32[]{:S(2)}) async-start(f32[16,40,128]{2,1,0:T(8,128)} %get-tuple-element.45), calls=%async_computation.3 | async-start | bytes 655360 | tf_op jit(solution)/shard_map/all_to_all | solution.py:148
  486.6 58.0 %all-to-all-start = ((f32[16,40,128]{2,1,0:T(8,128)}), f32[16,40,128]{2,1,0:T(8,128)S(1)}, u32[]{:S(2)}, u32[]{:S(2)}) async-start(f32[16,40,128]{2,1,0:T(8,128)} %get-tuple-element.43), calls=%async_computation | async-start | bytes 655360 | tf_op jit(solution)/shard_map/all_to_all | solution.py:145
  491.7 46.6 %copy-start.4 = (s32[8192]{0:T(1024)S(1)}, s32[8192]{0:T(1024)}, u32[]{:S(2)}) copy-start(s32[8192]{0:T(1024)} %param.16) | copy-start | bytes 98308
  491.7 46.6 %copy-start.9 = (s32[8192,1]{0,1:T(1,128)S(1)}, s32[8192,1]{0,1:T(1,128)}, u32[]{:S(2)}) copy-start(s32[8192,1]{0,1:T(1,128)} %get-tuple-element.35) | copy-start | bytes 98308
  544.6 68.0 %all-to-all-start.1 = ((f32[16,40,128]{2,1,0:T(8,128)}), f32[16,40,128]{2,1,0:T(8,128)S(1)}, u32[]{:S(2)}, u32[]{:S(2)}) async-start(f32[16,40,128]{2,1,0:T(8,128)} %get-tuple-element.44), calls=%async_computation.2 | async-start | bytes 655360 | tf_op jit(solution)/shard_map/all_to_all | solution.py:142
Sparse Core Ops, SparseCore 0:
  116.0 97.8 reduce-scatter.1
  216.7 60.2 all-gather.3
  443.2 20.5 all-reduce.1
  466.6 55.9 all-gather.5
